TPU v7x, 256 devices: a whole 4x4x8 slice. The times are simulated.
256 devices in a mesh: pix: 64 (over z, y, core), band: 4 (over x).
Axes of the slice: x: 4, y: 4, z: 8, core: 2. Of those that a mesh axis runs over, the one named last changes fastest.
Arguments:
- series: bfloat16 [224, 128, 16384], P('band', None, 'pix'), may hold values from 0 to 1
- pixel_factor: float32 [64, 16384], P(None, 'pix'), may hold values from 0.03 to 0.6
- band_factor: float32 [224, 64], P('band'), may hold values from 0.03 to 0.6
- time_factor: float32 [128, 64], replicated, may hold values from 0.03 to 0.6
Outputs:
- pixels_out: float32 [64, 16384], P(None, 'pix')
- bands_out: float32 [224, 64], P('band')
- times_out: float32 [128, 64], replicated
All inputs are finite; a program needn't handle non-finite values.
Results may differ from a plain program's by a relative error of at most 0.00045.
Values sent between devices are 32-bit elements; how exact they have to be, the bound alone decides.
A program may use at most 64 MiB of HBM per device.

v0:
```python
import jax
import jax.numpy as jnp
from jax import lax
from jax.sharding import PartitionSpec as P

SWEEPS = 4


HIGH = lax.Precision.HIGHEST


def step_of(gram):
    return 1.0 / (jnp.max(jnp.sum(gram, axis=1)) + 1e-06)


def band_gram_of(bands):
    local_gram = jnp.dot(bands.T, bands, precision=HIGH, preferred_element_type=jnp.float32)
    return lax.psum(local_gram, "band")


def body(series, pixel_factor, band_factor, time_factor):
    pixels = pixel_factor
    bands = band_factor
    times = time_factor
    gram_b = band_gram_of(bands)
    for sweep in range(SWEEPS):
        gram_c = jnp.dot(times.T, times, precision=HIGH, preferred_element_type=jnp.float32)
        c_low = times.astype(jnp.bfloat16)
        folded = jnp.einsum("btp,tr->brp", series, c_low, preferred_element_type=jnp.float32)
        partial_a = jnp.einsum("brp,br->rp", folded, bands, precision=HIGH)
        gram = gram_b * gram_c
        scale = step_of(gram)
        target = lax.psum(partial_a, "band")
        pixels = jnp.maximum(pixels - scale * (jnp.dot(gram, pixels, precision=HIGH) - target), 0.0)
        local_gram = jnp.dot(pixels, pixels.T, precision=HIGH, preferred_element_type=jnp.float32)
        partial_b = jnp.einsum("brp,rp->br", folded, pixels, precision=HIGH)
        gram_a = lax.psum(local_gram, "pix")
        target_b = lax.psum(partial_b, "pix")
        gram = gram_a * gram_c
        bands = jnp.maximum(
            bands - step_of(gram) * (jnp.dot(bands, gram, precision=HIGH) - target_b), 0.0
        )
        gram_b = band_gram_of(bands)
        p_low = pixels.astype(jnp.bfloat16)
        b_low = bands.astype(jnp.bfloat16).astype(jnp.float32)
        spread = jnp.einsum("btp,rp->brt", series, p_low, preferred_element_type=jnp.float32)
        partial_c = jnp.einsum("brt,br->tr", spread, b_low, precision=HIGH)
        target_c = lax.psum(partial_c, ("pix", "band"))
        gram = gram_a * gram_b
        times = jnp.maximum(
            times - step_of(gram) * (jnp.dot(times, gram, precision=HIGH) - target_c), 0.0
        )
    return (pixels, bands, times)


def solution(mesh):
    placed = (P("band", None, "pix"), P(None, "pix"), P("band", None), P())
    return jax.shard_map(
        body,
        mesh=mesh,
        in_specs=placed,
        out_specs=(P(None, "pix"), P("band", None), P()),
        check_vma=False,
    )
```

profile of v0, /device:TPU:1, one launch (start us, length us, event | category | flops | bytes accessed | tf_op | source)
XLA Modules:
  0.0 1634.8 jit_solution(12999607043672692766)
XLA Ops:
  8.0 2.7 convolution_bitcast_fusion.3
  12.5 4.1 fusion.14
  17.8 14.4 psum.147
  33.7 31.5 %all-reduce.9.cloned.1.call-done = f32[64,256]{1,0:T(8,128)} async-done(((f32[64,256]{1,0:T(8,128)}), f32[64,256]{1,0:T(8,128)}) %all-reduce.9.cloned.1.call-update) | async-done | bytes 65552 | tf_op jit(solution)/shard_map/psum | solution.py:33
  66.5 3.3 fusion.76
  69.8 4.9 fusion.12
  74.8 246.3 %all-reduce.3 = (f32[56,64]{1,0:T(8,128)S(1)}, f32[64,64]{0,1:T(8,128)S(1)}) all-reduce(f32[56,64]{1,0:T(8,128)S(1)} %bitcast.190, f32[64,64]{0,1:T(8,128)S(1)} %fusion.104), channel_id=1, replica_groups=mesh['pix'=64,'band'=4] {'pix'}, use_global_device_ids=true, to_apply=%region_7.0 | all-reduce | flops 7680 | bytes 61440 | tf_op jit(solution)/shard_map/psum | solution.py:38
  325.1 77.7 %psum.152 = f32[128,64]{0,1:T(8,128)S(1)} all-reduce(f32[128,64]{0,1:T(8,128)S(1)} %bitcast.186), channel_id=1, replica_groups=mesh['pix'=64,'band'=4] {'pix','band'}, use_global_device_ids=true, to_apply=%region_11.0 | all-reduce | flops 8192 | bytes 65536 | tf_op jit(solution)/shard_map/psum | solution.py:48
  402.7 12.0 psum.151
  416.2 2.7 convolution_bitcast_fusion.2
  420.7 4.1 fusion.10
  427.4 41.3 %all-reduce.11.cloned.1.call-done = f32[64,256]{1,0:T(8,128)} async-done(((f32[64,256]{1,0:T(8,128)}), f32[64,256]{1,0:T(8,128)}) %all-reduce.11.cloned.1.call-update) | async-done | bytes 65552 | tf_op jit(solution)/shard_map/psum | solution.py:33
  470.2 3.3 fusion.74
  473.4 4.9 fusion.8
  478.5 246.1 %all-reduce.2 = (f32[56,64]{1,0:T(8,128)S(1)}, f32[64,64]{0,1:T(8,128)S(1)}) all-reduce(f32[56,64]{1,0:T(8,128)S(1)} %bitcast.191, f32[64,64]{0,1:T(8,128)S(1)} %fusion.106), channel_id=1, replica_groups=mesh['pix'=64,'band'=4] {'pix'}, use_global_device_ids=true, to_apply=%region_18.0 | all-reduce | flops 7680 | bytes 61440 | tf_op jit(solution)/shard_map/psum | solution.py:38
  728.5 77.7 %psum.157 = f32[128,64]{0,1:T(8,128)S(1)} all-reduce(f32[128,64]{0,1:T(8,128)S(1)} %bitcast.187), channel_id=1, replica_groups=mesh['pix'=64,'band'=4] {'pix','band'}, use_global_device_ids=true, to_apply=%region_22.0 | all-reduce | flops 8192 | bytes 65536 | tf_op jit(solution)/shard_map/psum | solution.py:48
  806.2 12.2 psum.156
  824.4 4.1 fusion.6
  830.6 41.8 %all-reduce.13.cloned.1.call-done = f32[64,256]{1,0:T(8,128)} async-done(((f32[64,256]{1,0:T(8,128)}), f32[64,256]{1,0:T(8,128)}) %all-reduce.13.cloned.1.call-update) | async-done | bytes 65552 | tf_op jit(solution)/shard_map/psum | solution.py:33
  873.9 3.3 fusion.72
  877.2 4.9 fusion.4
  882.2 246.3 %all-reduce.1 = (f32[56,64]{1,0:T(8,128)S(1)}, f32[64,64]{0,1:T(8,128)S(1)}) all-reduce(f32[56,64]{1,0:T(8,128)S(1)} %bitcast.192, f32[64,64]{0,1:T(8,128)S(1)} %fusion.108), channel_id=1, replica_groups=mesh['pix'=64,'band'=4] {'pix'}, use_global_device_ids=true, to_apply=%region_29.0 | all-reduce | flops 7680 | bytes 61440 | tf_op jit(solution)/shard_map/psum | solution.py:38
  1132.5 77.7 %psum.162 = f32[128,64]{0,1:T(8,128)S(1)} all-reduce(f32[128,64]{0,1:T(8,128)S(1)} %bitcast.188), channel_id=1, replica_groups=mesh['pix'=64,'band'=4] {'pix','band'}, use_global_device_ids=true, to_apply=%region_33.0 | all-reduce | flops 8192 | bytes 65536 | tf_op jit(solution)/shard_map/psum | solution.py:48
  1210.1 12.0 psum.161
  1223.6 2.7 convolution_bitcast_fusion
  1228.1 4.1 fusion.2
  1234.3 41.8 %all-reduce.15.cloned.1.call-done = f32[64,256]{1,0:T(8,128)} async-done(((f32[64,256]{1,0:T(8,128)}), f32[64,256]{1,0:T(8,128)}) %all-reduce.15.cloned.1.call-update) | async-done | bytes 65552 | tf_op jit(solution)/shard_map/psum | solution.py:33
  1277.6 3.3 fusion.70
  1280.9 4.9 fusion
  1285.9 246.3 %all-reduce = (f32[56,64]{1,0:T(8,128)S(1)}, f32[64,64]{0,1:T(8,128)S(1)}) all-reduce(f32[56,64]{1,0:T(8,128)S(1)} %bitcast.193, f32[64,64]{0,1:T(8,128)S(1)} %fusion.110), channel_id=1, replica_groups=mesh['pix'=64,'band'=4] {'pix'}, use_global_device_ids=true, to_apply=%region_40.0 | all-reduce | flops 7680 | bytes 61440 | tf_op jit(solution)/shard_map/psum | solution.py:38
  1536.1 77.7 %psum.167 = f32[128,64]{0,1:T(8,128)S(1)} all-reduce(f32[128,64]{0,1:T(8,128)S(1)} %bitcast.189), channel_id=1, replica_groups=mesh['pix'=64,'band'=4] {'pix','band'}, use_global_device_ids=true, to_apply=%region_44.0 | all-reduce | flops 8192 | bytes 65536 | tf_op jit(solution)/shard_map/psum | solution.py:48
  1613.8 12.0 psum.166
  (106 shorter events, 40.2 us)
Async XLA Ops:
  7.2 58.0 %all-reduce.9.cloned.1.call-start = ((), (), s32[]{:S(2)}) async-start(), calls=%async_computation | async-start | bytes 131072 | tf_op jit(solution)/shard_map/psum | solution.py:33
  10.7 1.8 copy-start
  12.5 4.8 copy-start.10
  12.5 5.0 copy-start.9
  12.5 52.6 %copy-start.12 = (f32[64,256]{1,0:T(8,128)S(1)}, f32[64,256]{1,0:T(8,128)}, u32[]{:S(2)}) copy-start(f32[64,256]{1,0:T(8,128)} %param.5) | copy-start | bytes 196612
  17.3 451.4 %all-reduce.11.cloned.1.call-start = ((), (), s32[]{:S(2)}) async-start(), calls=%async_computation.1 | async-start | bytes 131072 | tf_op jit(solution)/shard_map/psum | solution.py:33
  65.1 4.7 copy-start.1
  418.9 1.8 copy-start.2
  425.4 447.1 %all-reduce.13.cloned.1.call-start = ((), (), s32[]{:S(2)}) async-start(), calls=%async_computation.2 | async-start | bytes 131072 | tf_op jit(solution)/shard_map/psum | solution.py:33
  468.7 4.7 copy-start.3
  822.6 1.8 copy-start.4
  829.1 447.0 %all-reduce.15.cloned.1.call-start = ((), (), s32[]{:S(2)}) async-start(), calls=%async_computation.3 | async-start | bytes 131072 | tf_op jit(solution)/shard_map/psum | solution.py:33
  872.5 4.7 copy-start.5
  1226.3 1.8 copy-start.6
  1276.1 4.7 copy-start.7
  1277.4 8.4 copy-start.8
  1533.8 94.1 %copy-start.11 = (f32[56,64]{1,0:T(8,128)}, f32[56,64]{1,0:T(8,128)S(1)}, u32[]{:S(2)}) copy-start(f32[56,64]{1,0:T(8,128)S(1)} %fusion.55) | copy-start | bytes 43012
Sparse Core Ops, SparseCore 0:
  17.4 47.6 all-reduce.8
  425.5 43.1 all-reduce.10
  829.2 43.2 all-reduce.12
  1232.9 43.1 all-reduce.14
where the time goes:
time: 1650 us; the launch traced here: 1630 us
  blocking collectives  1360 us (82%)
  waiting for transfers between devices  157 us (10%)
  matrix products  77.5 us (5%)
  between operations  22.9 us (1%)
    psum x4, blocking collectives, body(): target_b = lax.psum(partial_b, 'pix')  985 us
    psum x4, blocking collectives, body(): target_c = lax.psum(partial_c, ('pix', 'band'))  311 us
    psum x4, waiting for transfers between devices, body(): target = lax.psum(partial_a, 'band')  156 us
    psum x5, blocking collectives, band_gram_of(): return lax.psum(local_gram, 'band')  62.4 us
  transfers between devices with their start and end apart: 4, of which 4 were waited for; matrix products, arithmetic and copies ran while one was open for 0% of the time, Pallas kernels for 0%

commit v1 on v0

v1 whole, which is shorter than its diff:
```python
import functools

import jax
import jax.numpy as jnp
from jax import lax
from jax.experimental import pallas as pl
from jax.experimental.pallas import tpu as pltpu
from jax.sharding import PartitionSpec as P

SWEEPS = 4
RANK = 64
LANES = 128
UNROLL = 8
F32 = jnp.float32
HIGH = lax.Precision.HIGHEST
MESH = pl.DeviceIdType.MESH

AT_PIXELS, AT_GRAM, B_SCATTER, B_Z, B_GATHER, C_SCATTER, C_Z, C_X, C_GATHER = range(9)


def dot_nn(a, b):
    return lax.dot_general(
        a, b, (((1,), (0,)), ((), ())), precision=HIGH, preferred_element_type=F32
    )


def dot_nt(a, b):
    return lax.dot_general(
        a, b, (((1,), (1,)), ((), ())), precision=HIGH, preferred_element_type=F32
    )


def padded_gram(a):
    return dot_nt(a, jnp.concatenate([a, jnp.zeros_like(a)], axis=0))


def step_of(gram):
    sums = jnp.sum(gram, axis=0, keepdims=True)
    return 1.0 / (jnp.max(sums, axis=1, keepdims=True) + 1e-06)


def total_of(slots):
    total = slots[0]
    for j in range(1, slots.shape[0]):
        total = total + slots[j]
    return total


def kernel(
    nx, nz, inner,
    series, pixels_in, bands_in, times_in,
    pixels, bands, times,
    gram_b, wide, folded, spread,
    a_slots, g_slots,
    b_send, b_parts, b_z, b_all,
    c_send, c_parts, c_z, c_x, c_all,
    send_sems, recv_sems,
):
    nb = series.shape[0]
    pix_me = lax.axis_index("pix")
    x_me = lax.axis_index("band")
    z_me = pix_me // inner
    i_me = lax.rem(pix_me, inner)

    def on_x(k):
        return (pix_me, k)

    def on_z(k):
        return (k * inner + i_me, x_me)

    def on_inner(k):
        return (z_me * inner + k, x_me)

    groups = ((on_x, x_me, nx), (on_z, z_me, nz), (on_inner, i_me, inner))
    barrier = pltpu.get_barrier_semaphore()
    for at, me, n in groups:
        for d in range(1, n):
            pl.semaphore_signal(
                barrier, inc=1, device_id=at(lax.rem(me + d, n)), device_id_type=MESH
            )
    pl.semaphore_wait(barrier, sum(n - 1 for _, _, n in groups))

    def copies_of(phase, group, source, slots, sent):
        at, me, n = group
        copies = []
        for d in range(1, n):
            to = lax.rem(me + d, n)
            slot = me if sent else lax.rem(me + n - d, n)
            copies.append(
                pltpu.make_async_remote_copy(
                    src_ref=slots.at[me] if source is None else source.at[to],
                    dst_ref=slots.at[slot],
                    send_sem=send_sems.at[phase, d],
                    recv_sem=recv_sems.at[phase, d],
                    device_id=at(to),
                    device_id_type=MESH,
                )
            )
        return copies

    def start(phase, group, source, slots):
        for copy in copies_of(phase, group, source, slots, True):
            copy.start()

    def finish(phase, group, source, slots):
        for copy in copies_of(phase, group, source, slots, False):
            copy.wait_recv()
        for copy in copies_of(phase, group, source, slots, True):
            copy.wait_send()

    x_group, z_group, in_group = groups
    lane = lax.broadcasted_iota(jnp.int32, (RANK, LANES), 1)

    def column(value, b):
        return jnp.broadcast_to(value[:, RANK + b : RANK + b + 1], (RANK, LANES))

    pixels[...] = pixels_in[...]
    times[...] = times_in[...]
    first = bands_in[...]
    bands[...] = first
    g_slots[x_me] = padded_gram(first)
    start(AT_GRAM, x_group, None, g_slots)
    for b in range(nb):
        wide[b] = column(first, b)
    finish(AT_GRAM, x_group, None, g_slots)
    gram_b[...] = total_of(g_slots)

    def sweep(_, carry):
        ct = times[...]
        gram_c = dot_nt(ct, ct)
        c_low = ct.astype(jnp.bfloat16)

        def fold(i, acc):
            for u in range(UNROLL):
                b = i * UNROLL + u
                one = jnp.dot(c_low, series[b], preferred_element_type=F32)
                folded[b] = one
                weight = wide[b]
                acc = acc + one * jnp.concatenate([weight, weight], axis=1)
            return acc

        a_slots[x_me] = lax.fori_loop(
            0, nb // UNROLL, fold, jnp.zeros(pixels.shape, F32)
        )
        start(AT_PIXELS, x_group, None, a_slots)
        gram = gram_b[...][:, :RANK] * gram_c
        scale = step_of(gram)
        p = pixels[...]
        moved = dot_nn(gram, p)
        finish(AT_PIXELS, x_group, None, a_slots)
        p = jnp.maximum(p - scale * (moved - total_of(a_slots)), 0.0)
        pixels[...] = p
        p_low = p.astype(jnp.bfloat16)

        def into_bands(i, acc):
            for u in range(UNROLL):
                b = i * UNROLL + u
                both = folded[b] * p
                half = both[:, :LANES] + both[:, LANES:]
                acc = jnp.where(
                    lane == RANK + b, jnp.sum(half, axis=1, keepdims=True), acc
                )
            return acc

        both = lax.fori_loop(0, nb // UNROLL, into_bands, padded_gram(p))
        b_send[...] = both.reshape(b_send.shape)
        b_parts[i_me] = b_send[i_me]

        def spread_over(low, high):
            def some(i, carry):
                for u in range(UNROLL):
                    b = i * UNROLL + u
                    spread[b] = lax.dot_general(
                        p_low, series[b], (((1,), (1,)), ((), ())),
                        preferred_element_type=F32,
                    )
                return carry

            lax.fori_loop(low, high, some, 0)

        blocks = nb // UNROLL
        cuts = (0, (blocks * 3 + 6) // 7, (blocks * 5 + 6) // 7, blocks)
        start(B_SCATTER, in_group, b_send, b_parts)
        spread_over(cuts[0], cuts[1])
        finish(B_SCATTER, in_group, b_send, b_parts)
        b_z[z_me] = total_of(b_parts)
        start(B_Z, z_group, None, b_z)
        spread_over(cuts[1], cuts[2])
        finish(B_Z, z_group, None, b_z)
        b_all[i_me] = total_of(b_z)
        start(B_GATHER, in_group, None, b_all)
        spread_over(cuts[2], cuts[3])
        finish(B_GATHER, in_group, None, b_all)
        both = b_all[...].reshape(RANK, LANES)
        gram_a = both[:, :RANK]
        target = jnp.where(lane >= RANK, both, 0.0)
        gram = gram_a * gram_c
        bt = bands[...]
        bt = jnp.maximum(bt - step_of(gram) * (dot_nn(gram, bt) - target), 0.0)
        bands[...] = bt
        g_slots[x_me] = padded_gram(bt)
        start(AT_GRAM, x_group, None, g_slots)

        acc = jnp.zeros((RANK, LANES), F32)
        for b in range(nb):
            weight = column(bt, b)
            wide[b] = weight
            acc = acc + spread[b] * weight.astype(jnp.bfloat16).astype(F32)
        c_send[...] = acc.reshape(c_send.shape)
        c_parts[i_me] = c_send[i_me]
        start(C_SCATTER, in_group, c_send, c_parts)
        finish(C_SCATTER, in_group, c_send, c_parts)
        c_z[z_me] = total_of(c_parts)
        start(C_Z, z_group, None, c_z)
        finish(AT_GRAM, x_group, None, g_slots)
        new_gram = total_of(g_slots)
        gram_b[...] = new_gram
        gram = gram_a * new_gram[:, :RANK]
        scale = step_of(gram)
        moved = dot_nn(gram, ct)
        finish(C_Z, z_group, None, c_z)
        c_x[x_me] = total_of(c_z)
        start(C_X, x_group, None, c_x)
        finish(C_X, x_group, None, c_x)
        c_all[i_me] = total_of(c_x)
        start(C_GATHER, in_group, None, c_all)
        finish(C_GATHER, in_group, None, c_all)
        target = c_all[...].reshape(RANK, LANES)
        times[...] = jnp.maximum(ct - scale * (moved - target), 0.0)
        return carry

    lax.fori_loop(0, SWEEPS, sweep, 0)


def body(nx, nz, inner, series, pixel_factor, band_factor, time_factor):
    nb = series.shape[0]
    rows = RANK // inner
    bands_in = jnp.pad(band_factor.T, ((0, 0), (RANK, LANES - RANK - nb)))
    vmem = pl.BlockSpec(memory_space=pltpu.VMEM)
    wide = (RANK, LANES)
    pixels, bands, times = pl.pallas_call(
        functools.partial(kernel, nx, nz, inner),
        out_shape=(
            jax.ShapeDtypeStruct(pixel_factor.shape, F32),
            jax.ShapeDtypeStruct(wide, F32),
            jax.ShapeDtypeStruct(wide, F32),
        ),
        in_specs=[vmem] * 4,
        out_specs=(vmem,) * 3,
        scratch_shapes=[
            pltpu.VMEM(wide, F32),
            pltpu.VMEM((nb,) + wide, F32),
            pltpu.VMEM((nb,) + pixel_factor.shape, F32),
            pltpu.VMEM((nb,) + wide, F32),
            pltpu.VMEM((nx,) + pixel_factor.shape, F32),
            pltpu.VMEM((nx,) + wide, F32),
            pltpu.VMEM((inner, rows, LANES), F32),
            pltpu.VMEM((inner, rows, LANES), F32),
            pltpu.VMEM((nz, rows, LANES), F32),
            pltpu.VMEM((inner, rows, LANES), F32),
            pltpu.VMEM((inner, rows, LANES), F32),
            pltpu.VMEM((inner, rows, LANES), F32),
            pltpu.VMEM((nz, rows, LANES), F32),
            pltpu.VMEM((nx, rows, LANES), F32),
            pltpu.VMEM((inner, rows, LANES), F32),
            pltpu.SemaphoreType.DMA((9, 8)),
            pltpu.SemaphoreType.DMA((9, 8)),
        ],
        compiler_params=pltpu.CompilerParams(collective_id=0, has_side_effects=True),
    )(series, pixel_factor, bands_in, time_factor.T)
    return pixels, bands[:, RANK : RANK + nb].T, times.T


def build(mesh, inner):
    placed = (P("band", None, "pix"), P(None, "pix"), P("band", None), P())
    return jax.shard_map(
        functools.partial(body, mesh.shape["band"], mesh.shape["pix"] // inner, inner),
        mesh=mesh,
        in_specs=placed,
        out_specs=(P(None, "pix"), P("band", None), P()),
        check_vma=False,
    )


def solution(mesh):
    return build(mesh, 8)
```

time: 1650 us -> 170 us (0.10)
  blocking collectives: 1360 us -> 0 us
  Pallas kernels: 0 us -> 163 us
  waiting for transfers between devices: 157 us -> 0 us
  matrix products: 77.5 us -> 0 us
  between operations: 22.9 us -> 0.64 us
    psum x13 -> x0, blocking collectives: 1360 us -> none  [the longest x4 985 us: body(): target_b = lax.psum(partial_b, 'pix')]
    pallas_call x0 -> x1, Pallas kernels: none -> 163 us  [body(): pl.pallas_call(functools.partial(kernel, nx, nz, inner), out_shape=(jax.S...]
    psum x4 -> x0, waiting for transfers between devices: 156 us -> none  [body(): target = lax.psum(partial_a, 'band')]
    dot_general x45 -> x0, matrix products: 77.5 us -> none  [the longest x4 19.8 us: body(): partial_b = jnp.einsum('brp,rp->br', folded, pixels, precision=HIGH)]
  transfers between devices with their start and end apart: 4 -> 0, of which waited for: 4 -> 0; matrix products, arithmetic and copies ran while one was open for 0% -> 0% of each run, Pallas kernels for 0% -> 0%
where the time goes in v1:
time: 170 us
  Pallas kernels  163 us (96%)
  local copies, waits for them, and re-layouts  5.9 us (3%)
    pallas_call x1, Pallas kernels, body(): pl.pallas_call(functools.partial(kernel, nx, nz, inner), out_shape=(jax.S...  163 us
    unnamed x4, local copies, waits for them, and re-layouts  4.36 us

profile of v1, /device:TPU:1, one launch (start us, length us, event | category | flops | bytes accessed | tf_op | source)
XLA Modules:
  0.0 169.9 jit_solution(6043947219800577526)
XLA Ops:
  0.6 0.8 copy.7
  1.5 0.7 pad.4.bands_in
  2.2 163.3 %shard_map.67 = (f32[64,256]{1,0:T(8,128)}, f32[64,128]{1,0:T(8,128)}, f32[64,128]{1,0:T(8,128)}) custom-call(bf16[56,128,256]{2,1,0:T(8,128)(2,1)} %series.1, f32[64,256]{1,0:T(8,128)} %pixels_in.1, f32[64,128]{1,0:T(8,128)} %pad.4.bands_in, f32[64,128]{1,0:T(8,128)} %bitcast.7), custom_call_target="tpu_custom_call" | custom-call | tf_op jit(solution)/shard_map/pallas_call | solution.py:241
  165.5 0.8 slice_bitcast_fusion
  166.3 0.7 copy.8
  167.0 1.5 copy.11
  168.5 1.4 copy.12

commit v2 on v1

v2 whole, which is shorter than its diff:
```python
import functools

import jax
import jax.numpy as jnp
from jax import lax
from jax.experimental import pallas as pl
from jax.experimental.pallas import tpu as pltpu
from jax.sharding import PartitionSpec as P

SWEEPS = 4
RANK = 64
LANES = 128
UNROLL = 8
F32 = jnp.float32
HIGH = lax.Precision.HIGHEST
MESH = pl.DeviceIdType.MESH

(
    AT_PIXELS, AT_GRAM, AT_FIRST, B_PAIR, B_Y, B_Z, B_BACK,
    C_PAIR, C_Y, C_X, C_Z, C_BACK, PHASES,
) = range(13)
HALF = RANK // 2


def dot_nn(a, b):
    return lax.dot_general(
        a, b, (((1,), (0,)), ((), ())), precision=HIGH, preferred_element_type=F32
    )


def dot_nt(a, b):
    return lax.dot_general(
        a, b, (((1,), (1,)), ((), ())), precision=HIGH, preferred_element_type=F32
    )


def padded_gram(a):
    return dot_nt(a, jnp.concatenate([a, jnp.zeros_like(a)], axis=0))


def step_of(gram):
    sums = jnp.sum(gram, axis=0, keepdims=True)
    return 1.0 / (jnp.max(sums, axis=1, keepdims=True) + 1e-06)


def total_of(slots):
    total = slots[0]
    for j in range(1, slots.shape[0]):
        total = total + slots[j]
    return total


def kernel(
    nx, ny, nz,
    series_in, pixels_in, bands_in, times_in,
    pixels, bands_out, times,
    series, bands, gram_b, wide, folded, spread,
    a_slots, g_slots, first_slots,
    b_send, b_pair, b_y, b_z, b_all,
    c_send, c_pair, c_y, c_x, c_z, c_all,
    send_sems, recv_sems, load_sem,
):
    nb = series.shape[0]
    load = pltpu.make_async_copy(series_in, series, load_sem)
    load.start()
    pix_me = lax.axis_index("pix")
    x_me = lax.axis_index("band")
    z_me = pix_me // (2 * ny)
    y_me = lax.rem(pix_me // 2, ny)
    c_me = lax.rem(pix_me, 2)

    def on_x(k):
        return (pix_me, k)

    def on_z(k):
        return (k * (2 * ny) + y_me * 2 + c_me, x_me)

    def on_y(k):
        return (z_me * (2 * ny) + k * 2 + c_me, x_me)

    def on_core(k):
        return (z_me * (2 * ny) + y_me * 2 + k, x_me)

    groups = ((on_x, x_me, nx), (on_z, z_me, nz), (on_y, y_me, ny), (on_core, c_me, 2))
    x_group, z_group, y_group, core_group = groups
    barrier = pltpu.get_barrier_semaphore()
    for at, me, n in groups:
        for d in range(1, n):
            pl.semaphore_signal(
                barrier, inc=1, device_id=at(lax.rem(me + d, n)), device_id_type=MESH
            )
    pl.semaphore_wait(barrier, sum(n - 1 for _, _, n in groups))

    def copies_of(phase, group, source, slots, sent):
        at, me, n = group
        copies = []
        for d in sorted(range(1, n), key=lambda d: -min(d, n - d)):
            to = lax.rem(me + d, n)
            slot = me if sent else lax.rem(me + n - d, n)
            copies.append(
                pltpu.make_async_remote_copy(
                    src_ref=slots.at[me] if source is None else source,
                    dst_ref=slots if source is not None else slots.at[slot],
                    send_sem=send_sems.at[phase, d],
                    recv_sem=recv_sems.at[phase, d],
                    device_id=at(to),
                    device_id_type=MESH,
                )
            )
        return copies

    def start(phase, group, slots, source=None):
        for copy in copies_of(phase, group, source, slots, True):
            copy.start()

    def arrived(phase, group, slots, source=None):
        for copy in copies_of(phase, group, source, slots, False):
            copy.wait_recv()

    def sent(phase, group, slots, source=None):
        for copy in copies_of(phase, group, source, slots, True):
            copy.wait_send()

    lane = lax.broadcasted_iota(jnp.int32, (RANK, LANES), 1)
    half_lane = lax.broadcasted_iota(jnp.int32, (HALF, LANES), 1)
    mine = pl.multiple_of(c_me * HALF, HALF)
    other = pl.multiple_of((1 - c_me) * HALF, HALF)

    def column(value, b):
        one = value[:, RANK + b : RANK + b + 1]
        return jnp.broadcast_to(one, (value.shape[0], LANES))

    rest = LANES - RANK - nb
    tall = [jnp.zeros((RANK, RANK), F32), bands_in[...]]
    if rest:
        tall.append(jnp.zeros((rest, RANK), F32))
    unit = (
        lax.broadcasted_iota(jnp.int32, (RANK, RANK), 0)
        == lax.broadcasted_iota(jnp.int32, (RANK, RANK), 1)
    ).astype(F32)
    first = dot_nt(unit, jnp.concatenate(tall, axis=0))
    bands[...] = first
    first_slots[x_me] = padded_gram(first)
    start(AT_FIRST, x_group, first_slots)
    pixels[...] = pixels_in[...]
    times[...] = times_in[...]
    for b in range(nb):
        wide[b] = column(first, b)
    load.wait()

    def sweep(number, carry):
        ct = times[...]
        c_low = ct.astype(jnp.bfloat16)

        def fold(i, acc):
            for u in range(UNROLL):
                b = i * UNROLL + u
                one = jnp.dot(c_low, series[b], preferred_element_type=F32)
                folded[b] = one
                weight = wide[b]
                acc = acc + one * jnp.concatenate([weight, weight], axis=1)
            return acc

        acc = lax.fori_loop(0, nb // UNROLL, fold, jnp.zeros(pixels.shape, F32))
        a_slots[x_me] = acc
        start(AT_PIXELS, x_group, a_slots)

        @pl.when(number == 0)
        def _():
            arrived(AT_FIRST, x_group, first_slots)
            sent(AT_FIRST, x_group, first_slots)
            gram_b[...] = total_of(first_slots)

        gram_c = dot_nt(ct, ct)
        gram = gram_b[...][:, :RANK] * gram_c
        scale = step_of(gram)
        p = pixels[...]
        moved = p - scale * dot_nn(gram, p)
        arrived(AT_PIXELS, x_group, a_slots)
        p = jnp.maximum(moved + scale * total_of(a_slots), 0.0)
        pixels[...] = p
        p_low = p.astype(jnp.bfloat16)
        p_tall = jnp.concatenate([p, jnp.zeros_like(p)], axis=0)

        def band_part(low):
            rows = pl.ds(low, HALF)
            p_rows = pixels[rows, :]

            def into_bands(i, acc):
                for u in range(UNROLL):
                    b = i * UNROLL + u
                    both = folded[b, rows, :] * p_rows
                    both = both[:, :LANES] + both[:, LANES:]
                    acc = jnp.where(
                        half_lane == RANK + b,
                        jnp.sum(both, axis=1, keepdims=True), acc,
                    )
                return acc

            return lax.fori_loop(0, nb // UNROLL, into_bands, dot_nt(p_rows, p_tall))

        def spread_over(low, high):
            def some(i, carry):
                for u in range(UNROLL):
                    b = i * UNROLL + u
                    spread[b] = lax.dot_general(
                        p_low, series[b], (((1,), (1,)), ((), ())),
                        preferred_element_type=F32,
                    )
                return carry

            lax.fori_loop(low, high, some, 0)

        blocks = nb // UNROLL
        cuts = (0, (blocks + 6) // 7, (blocks * 4 + 6) // 7, blocks)
        b_send[...] = band_part(other)
        start(B_PAIR, core_group, b_pair, b_send)
        own = band_part(mine)
        sent(AT_PIXELS, x_group, a_slots)
        spread_over(cuts[0], cuts[1])
        arrived(B_PAIR, core_group, b_pair, b_send)
        b_y[y_me] = own + b_pair[...]
        start(B_Y, y_group, b_y)
        sent(B_PAIR, core_group, b_pair, b_send)
        spread_over(cuts[1], cuts[2])
        arrived(B_Y, y_group, b_y)
        b_z[z_me] = total_of(b_y)
        start(B_Z, z_group, b_z)
        sent(B_Y, y_group, b_y)
        spread_over(cuts[2], cuts[3])
        arrived(B_Z, z_group, b_z)
        b_all[c_me] = total_of(b_z)
        start(B_BACK, core_group, b_all)
        sent(B_Z, z_group, b_z)
        arrived(B_BACK, core_group, b_all)
        both = b_all[...].reshape(RANK, LANES)
        gram_a = both[:, :RANK]
        target = jnp.where(lane >= RANK, both, 0.0)
        gram = gram_a * gram_c
        bt = bands[...]
        bt = jnp.maximum(bt - step_of(gram) * (dot_nn(gram, bt) - target), 0.0)
        bands[...] = bt

        def time_part(low):
            rows = pl.ds(low, HALF)
            bt_rows = bands[rows, :]
            acc = jnp.zeros((HALF, LANES), F32)
            for b in range(nb):
                weight = column(bt_rows, b)
                wide[b, rows, :] = weight
                weight = weight.astype(jnp.bfloat16).astype(F32)
                acc = acc + spread[b, rows, :] * weight
            return acc

        c_send[...] = time_part(other)
        start(C_PAIR, core_group, c_pair, c_send)
        sent(B_BACK, core_group, b_all)
        g_slots[x_me] = padded_gram(bt)
        start(AT_GRAM, x_group, g_slots)
        own = time_part(mine)
        arrived(C_PAIR, core_group, c_pair, c_send)
        c_y[y_me] = own + c_pair[...]
        start(C_Y, y_group, c_y)
        sent(C_PAIR, core_group, c_pair, c_send)
        arrived(C_Y, y_group, c_y)
        c_x[x_me] = total_of(c_y)
        start(C_X, x_group, c_x)
        sent(C_Y, y_group, c_y)
        arrived(C_X, x_group, c_x)
        c_z[z_me] = total_of(c_x)
        start(C_Z, z_group, c_z)
        sent(C_X, x_group, c_x)
        arrived(AT_GRAM, x_group, g_slots)
        sent(AT_GRAM, x_group, g_slots)
        new_gram = total_of(g_slots)
        gram_b[...] = new_gram
        gram = gram_a * new_gram[:, :RANK]
        scale = step_of(gram)
        moved = ct - scale * dot_nn(gram, ct)
        arrived(C_Z, z_group, c_z)
        c_all[c_me] = total_of(c_z)
        start(C_BACK, core_group, c_all)
        sent(C_Z, z_group, c_z)
        arrived(C_BACK, core_group, c_all)
        target = c_all[...].reshape(RANK, LANES)
        times[...] = jnp.maximum(moved + scale * target, 0.0)
        sent(C_BACK, core_group, c_all)
        return carry

    lax.fori_loop(0, SWEEPS, sweep, 0)
    pick = (
        lax.broadcasted_iota(jnp.int32, (nb, LANES), 1)
        == lax.broadcasted_iota(jnp.int32, (nb, LANES), 0) + RANK
    ).astype(F32)
    bands_out[...] = dot_nt(pick, bands[...])


def body(nx, ny, nz, series, pixel_factor, band_factor, time_factor):
    nb = series.shape[0]
    vmem = pl.BlockSpec(memory_space=pltpu.VMEM)
    wide = (RANK, LANES)
    half = (HALF, LANES)

    def f32(*shape):
        return pltpu.VMEM(shape, F32)

    pixels, bands, times = pl.pallas_call(
        functools.partial(kernel, nx, ny, nz),
        out_shape=(
            jax.ShapeDtypeStruct(pixel_factor.shape, F32),
            jax.ShapeDtypeStruct(band_factor.shape, F32),
            jax.ShapeDtypeStruct(wide, F32),
        ),
        in_specs=[pl.BlockSpec(memory_space=pltpu.HBM)] + [vmem] * 3,
        out_specs=(vmem,) * 3,
        scratch_shapes=[
            pltpu.VMEM(series.shape, series.dtype),
            f32(*wide),
            f32(*wide),
            f32(nb, *wide),
            f32(nb, *pixel_factor.shape),
            f32(nb, *wide),
            f32(nx, *pixel_factor.shape),
            f32(nx, *wide),
            f32(nx, *wide),
            f32(*half),
            f32(*half),
            f32(ny, *half),
            f32(nz, *half),
            f32(2, *half),
            f32(*half),
            f32(*half),
            f32(ny, *half),
            f32(nx, *half),
            f32(nz, *half),
            f32(2, *half),
            pltpu.SemaphoreType.DMA((PHASES, 8)),
            pltpu.SemaphoreType.DMA((PHASES, 8)),
            pltpu.SemaphoreType.DMA,
        ],
        compiler_params=pltpu.CompilerParams(collective_id=0, has_side_effects=True),
    )(series, pixel_factor, band_factor, time_factor.T)
    return pixels, bands, times.T


def build(mesh, ny):
    placed = (P("band", None, "pix"), P(None, "pix"), P("band", None), P())
    return jax.shard_map(
        functools.partial(body, mesh.shape["band"], ny, mesh.shape["pix"] // (2 * ny)),
        mesh=mesh,
        in_specs=placed,
        out_specs=(P(None, "pix"), P("band", None), P()),
        check_vma=False,
    )


def solution(mesh):
    return build(mesh, 4)
```

time: 170 us -> 151 us (0.89)
  Pallas kernels: 163 us -> 146 us
    pallas_call x1, Pallas kernels: 163 us -> 146 us  [body(): pl.pallas_call(functools.partial(kernel, nx, ny, nz), out_shape=(jax.Shap...]
    unnamed x4 -> x3, local copies, waits for them, and re-layouts: 4.36 us -> 4.21 us
where the time goes in v2:
time: 151 us
  Pallas kernels  146 us (97%)
  local copies, waits for them, and re-layouts  4.21 us (3%)
    pallas_call x1, Pallas kernels, body(): pl.pallas_call(functools.partial(kernel, nx, ny, nz), out_shape=(jax.Shap...  146 us
    unnamed x3, local copies, waits for them, and re-layouts  4.21 us

profile of v2, /device:TPU:1, one launch (start us, length us, event | category | flops | bytes accessed | tf_op | source)
XLA Modules:
  0.0 151.1 jit_solution(3288206227455974145)
XLA Ops:
  0.6 146.3 %shard_map.67 = (f32[64,256]{1,0:T(8,128)}, f32[56,64]{1,0:T(8,128)}, f32[64,128]{1,0:T(8,128)}) custom-call(bf16[56,128,256]{2,1,0:T(8,128)(2,1)} %series_in.1, f32[64,256]{1,0:T(8,128)} %pixels_in.1, f32[56,64]{1,0:T(8,128)} %bands_in.1, f32[64,128]{1,0:T(8,128)} %bitcast.2), custom_call_target="tpu_custom_call" | custom-call | tf_op jit(solution)/shard_map/pallas_call | solution.py:307
  146.9 1.5 copy.10
  148.4 1.4 copy.11
  149.7 1.4 copy.12

commit v3 on v2

--- a/solution.py
+++ b/solution.py
@@ -11,14 +11,15 @@
 RANK = 64
 LANES = 128
 UNROLL = 8
+LONG = 56
 F32 = jnp.float32
 HIGH = lax.Precision.HIGHEST
 MESH = pl.DeviceIdType.MESH
 
 (
-    AT_PIXELS, AT_GRAM, AT_FIRST, B_PAIR, B_Y, B_Z, B_BACK,
+    AT_OTHER, AT_MINE, AT_GRAM, AT_FIRST, B_PAIR, B_Y, B_Z, B_BACK,
     C_PAIR, C_Y, C_X, C_Z, C_BACK, PHASES,
-) = range(13)
+) = range(14)
 HALF = RANK // 2
 
 
@@ -153,17 +154,18 @@
         c_low = ct.astype(jnp.bfloat16)
 
         def fold(i, acc):
-            for u in range(UNROLL):
-                b = i * UNROLL + u
+            for u in range(LONG):
+                b = i * LONG + u
                 one = jnp.dot(c_low, series[b], preferred_element_type=F32)
                 folded[b] = one
                 weight = wide[b]
                 acc = acc + one * jnp.concatenate([weight, weight], axis=1)
             return acc
 
-        acc = lax.fori_loop(0, nb // UNROLL, fold, jnp.zeros(pixels.shape, F32))
+        acc = lax.fori_loop(0, nb // LONG, fold, jnp.zeros(pixels.shape, F32))
         a_slots[x_me] = acc
-        start(AT_PIXELS, x_group, a_slots)
+        start(AT_OTHER, x_group, a_slots.at[:, pl.ds(other, HALF), :])
+        start(AT_MINE, x_group, a_slots.at[:, pl.ds(mine, HALF), :])
 
         @pl.when(number == 0)
         def _():
@@ -175,20 +177,22 @@
         gram = gram_b[...][:, :RANK] * gram_c
         scale = step_of(gram)
         p = pixels[...]
-        moved = p - scale * dot_nn(gram, p)
-        arrived(AT_PIXELS, x_group, a_slots)
-        p = jnp.maximum(moved + scale * total_of(a_slots), 0.0)
-        pixels[...] = p
-        p_low = p.astype(jnp.bfloat16)
-        p_tall = jnp.concatenate([p, jnp.zeros_like(p)], axis=0)
-
-        def band_part(low):
+        pixels[...] = p - scale * dot_nn(gram, p)
+
+        def new_rows(phase, low):
             rows = pl.ds(low, HALF)
-            p_rows = pixels[rows, :]
+            slots = a_slots.at[:, rows, :]
+            arrived(phase, x_group, slots)
+            p_rows = jnp.maximum(pixels[rows, :] + scale * total_of(slots), 0.0)
+            pixels[rows, :] = p_rows
+            return p_rows
+
+        def band_part(low, p_rows):
+            rows = pl.ds(low, HALF)
 
             def into_bands(i, acc):
-                for u in range(UNROLL):
-                    b = i * UNROLL + u
+                for u in range(LONG):
+                    b = i * LONG + u
                     both = folded[b, rows, :] * p_rows
                     both = both[:, :LANES] + both[:, LANES:]
                     acc = jnp.where(
@@ -197,7 +201,7 @@
                     )
                 return acc
 
-            return lax.fori_loop(0, nb // UNROLL, into_bands, dot_nt(p_rows, p_tall))
+            return lax.fori_loop(0, nb // LONG, into_bands, jnp.zeros((HALF, LANES), F32))
 
         def spread_over(low, high):
             def some(i, carry):
@@ -213,10 +217,17 @@
 
         blocks = nb // UNROLL
         cuts = (0, (blocks + 6) // 7, (blocks * 4 + 6) // 7, blocks)
-        b_send[...] = band_part(other)
+        p_other = new_rows(AT_OTHER, other)
+        part = band_part(other, p_other)
+        p_mine = new_rows(AT_MINE, mine)
+        p = pixels[...]
+        p_low = p.astype(jnp.bfloat16)
+        p_tall = jnp.concatenate([p, jnp.zeros_like(p)], axis=0)
+        b_send[...] = part + dot_nt(p_other, p_tall)
         start(B_PAIR, core_group, b_pair, b_send)
-        own = band_part(mine)
-        sent(AT_PIXELS, x_group, a_slots)
+        own = band_part(mine, p_mine) + dot_nt(p_mine, p_tall)
+        sent(AT_OTHER, x_group, a_slots.at[:, pl.ds(other, HALF), :])
+        sent(AT_MINE, x_group, a_slots.at[:, pl.ds(mine, HALF), :])
         spread_over(cuts[0], cuts[1])
         arrived(B_PAIR, core_group, b_pair, b_send)
         b_y[y_me] = own + b_pair[...]

time: 151 us -> 146 us (0.967)
  Pallas kernels: 146 us -> 141 us
    pallas_call x1, Pallas kernels: 146 us -> 141 us  [body(): pl.pallas_call(functools.partial(kernel, nx, ny, nz), out_shape=(jax.Shap...]
where the time goes in v3:
time: 146 us; the launch traced here: 145 us
  Pallas kernels  141 us (97%)
  local copies, waits for them, and re-layouts  4.21 us (3%)
    pallas_call x1, Pallas kernels, body(): pl.pallas_call(functools.partial(kernel, nx, ny, nz), out_shape=(jax.Shap...  141 us
    unnamed x3, local copies, waits for them, and re-layouts  4.21 us

profile of v3, /device:TPU:1, one launch (start us, length us, event | category | flops | bytes accessed | tf_op | source)
XLA Modules:
  0.0 145.5 jit_solution(12126013723336141932)
XLA Ops:
  0.6 140.6 %shard_map.67 = (f32[64,256]{1,0:T(8,128)}, f32[56,64]{1,0:T(8,128)}, f32[64,128]{1,0:T(8,128)}) custom-call(bf16[56,128,256]{2,1,0:T(8,128)(2,1)} %series_in.1, f32[64,256]{1,0:T(8,128)} %pixels_in.1, f32[56,64]{1,0:T(8,128)} %bands_in.1, f32[64,128]{1,0:T(8,128)} %bitcast.2), custom_call_target="tpu_custom_call" | custom-call | tf_op jit(solution)/shard_map/pallas_call | solution.py:318
  141.3 1.5 %copy.10 = f32[64,256]{1,0:T(8,128)} copy(f32[64,256]{1,0:T(8,128)} %get-tuple-element.12) | data formatting | bytes 131072
  142.7 1.4 copy.11
  144.1 1.4 copy.12

commit v4 on v3

--- a/solution.py
+++ b/solution.py
@@ -216,7 +216,7 @@
             lax.fori_loop(low, high, some, 0)
 
         blocks = nb // UNROLL
-        cuts = (0, (blocks + 6) // 7, (blocks * 4 + 6) // 7, blocks)
+        cut = (blocks * 4 + 6) // 7
         p_other = new_rows(AT_OTHER, other)
         part = band_part(other, p_other)
         p_mine = new_rows(AT_MINE, mine)
@@ -228,17 +228,16 @@
         own = band_part(mine, p_mine) + dot_nt(p_mine, p_tall)
         sent(AT_OTHER, x_group, a_slots.at[:, pl.ds(other, HALF), :])
         sent(AT_MINE, x_group, a_slots.at[:, pl.ds(mine, HALF), :])
-        spread_over(cuts[0], cuts[1])
         arrived(B_PAIR, core_group, b_pair, b_send)
         b_y[y_me] = own + b_pair[...]
         start(B_Y, y_group, b_y)
         sent(B_PAIR, core_group, b_pair, b_send)
-        spread_over(cuts[1], cuts[2])
+        spread_over(0, cut)
         arrived(B_Y, y_group, b_y)
         b_z[z_me] = total_of(b_y)
         start(B_Z, z_group, b_z)
         sent(B_Y, y_group, b_y)
-        spread_over(cuts[2], cuts[3])
+        spread_over(cut, blocks)
         arrived(B_Z, z_group, b_z)
         b_all[c_me] = total_of(b_z)
         start(B_BACK, core_group, b_all)

time: 146 us -> 145 us (level)
  no operation moved by 1% of the time
where the time goes in v4:
time: 145 us
  Pallas kernels  140 us (97%)
  local copies, waits for them, and re-layouts  4.21 us (3%)
    pallas_call x1, Pallas kernels, body(): pl.pallas_call(functools.partial(kernel, nx, ny, nz), out_shape=(jax.Shap...  140 us
    unnamed x3, local copies, waits for them, and re-layouts  4.21 us

profile of v4, /device:TPU:1, one launch (start us, length us, event | category | flops | bytes accessed | tf_op | source)
XLA Modules:
  0.0 145.0 jit_solution(7572608891207598441)
XLA Ops:
  0.6 140.2 %shard_map.67 = (f32[64,256]{1,0:T(8,128)}, f32[56,64]{1,0:T(8,128)}, f32[64,128]{1,0:T(8,128)}) custom-call(bf16[56,128,256]{2,1,0:T(8,128)(2,1)} %series_in.1, f32[64,256]{1,0:T(8,128)} %pixels_in.1, f32[56,64]{1,0:T(8,128)} %bands_in.1, f32[64,128]{1,0:T(8,128)} %bitcast.2), custom_call_target="tpu_custom_call" | custom-call | tf_op jit(solution)/shard_map/pallas_call | solution.py:317
  140.8 1.5 %copy.10 = f32[64,256]{1,0:T(8,128)} copy(f32[64,256]{1,0:T(8,128)} %get-tuple-element.12) | data formatting | bytes 131072
  142.3 1.4 copy.11
  143.7 1.4 copy.12
